TPU v7x, 32 devices: a whole 2x2x4 slice. The times are simulated.
32 devices in a mesh: seq: 16 (over z, x, core), head: 2 (over y).
Axes of the slice: x: 2, y: 2, z: 4, core: 2. Of those that a mesh axis runs over, the one named last changes fastest.
Arguments:
- queries: bfloat16 [2, 1024, 4096], P(None, ('seq', 'head')), may hold values from -6 to 6
- keys: bfloat16 [2, 1024, 4096], P(None, ('seq', 'head')), may hold values from -6 to 6
- values: bfloat16 [2, 1024, 4096], P(None, ('seq', 'head')), may hold values from -6 to 6
- rates: bfloat16 [2, 1024, 8], P(None, ('seq', 'head')), may hold values from 0.049804688 to 1
- fast_init: float32 [8, 3, 512, 256], P('head', None, 'seq'), may hold values from -0.25 to 0.25
Outputs:
- outputs: bfloat16 [2, 1024, 4096], P(None, 'seq', 'head')
All inputs are finite; a program needn't handle non-finite values.
Results may differ from a plain program's by a relative error of at most 0.0085.
Values may be sent and summed in bfloat16 or wider, within the bound.
No kernel may reach another device: no remote copies, remote signals or barrier semaphores. Data moves between devices by JAX's collectives and lax.ppermute only.
A program may use at most 64 MiB of HBM per device.

v0:
```python
import jax
import jax.numpy as jnp
from jax import lax
from jax.sharding import PartitionSpec as P

EPSILON = 1e-06
COEF_A = 3.4445
COEF_B = -4.775
COEF_C = 2.0315
LEARNING_STEP = 0.5
FULL_PRECISION = lax.Precision.HIGHEST


def silu_parts(gate_pre):
    sigmoid_value = jax.nn.sigmoid(gate_pre)
    return (gate_pre * sigmoid_value, sigmoid_value * (1.0 + gate_pre * (1.0 - sigmoid_value)))


def local_gram(weight_matrices):
    return jnp.einsum("hmrf,hmrg->hmfg", weight_matrices, weight_matrices, precision=FULL_PRECISION)


def newton_schulz(gradients, gram_fn):
    gram_matrix = gram_fn(gradients)
    norm_value = jnp.sqrt(jnp.trace(gram_matrix, axis1=2, axis2=3)) + EPSILON
    current_weights = gradients / norm_value[:, :, None, None]
    gram_matrix = gram_matrix / (norm_value * norm_value)[:, :, None, None]
    identity = jnp.eye(gram_matrix.shape[-1], dtype=gram_matrix.dtype)
    for sweeps in range(2):
        if sweeps > 0:
            gram_matrix = gram_fn(current_weights)
        square = jnp.einsum("hmfg,hmgk->hmfk", gram_matrix, gram_matrix, precision=FULL_PRECISION)
        polynomial_update = COEF_A * identity + COEF_B * gram_matrix + COEF_C * square
        current_weights = jnp.einsum(
            "hmrf,hmfg->hmrg", current_weights, polynomial_update, precision=FULL_PRECISION
        )
    return current_weights


def local(queries, keys, values, rates, fast_init):
    weights = lax.all_gather(fast_init, "seq", axis=2, tiled=True)
    head_count = weights.shape[0]
    head_size = weights.shape[2]
    results = []
    for group_index in range(queries.shape[0]):
        query_flat, key_flat, value_flat, rate_rows = (
            lax.all_to_all(queries[group_index], "head", split_axis=1, concat_axis=0, tiled=True),
            lax.all_to_all(keys[group_index], "head", split_axis=1, concat_axis=0, tiled=True),
            lax.all_to_all(values[group_index], "head", split_axis=1, concat_axis=0, tiled=True),
            lax.all_to_all(rates[group_index], "head", split_axis=1, concat_axis=0, tiled=True),
        )
        row_count = query_flat.shape[0]
        query_rows = query_flat.reshape(row_count, head_count, head_size)
        key_rows = key_flat.reshape(row_count, head_count, head_size)
        value_rows = value_flat.reshape(row_count, head_count, head_size)
        low = weights.astype(jnp.bfloat16)
        gate_pre = jnp.einsum(
            "rhd,hdf->rhf", key_rows, low[:, 0], preferred_element_type=jnp.float32
        )
        up_proj = jnp.einsum(
            "rhd,hdf->rhf", key_rows, low[:, 1], preferred_element_type=jnp.float32
        )
        activated_hidden, slope_value = silu_parts(gate_pre)
        hidden = (activated_hidden * up_proj).astype(jnp.bfloat16)
        out_grad = (
            -(rate_rows.astype(jnp.float32)[:, :, None] * value_rows.astype(jnp.float32))
        ).astype(jnp.bfloat16)
        hidden_grad = jnp.einsum(
            "rhd,hdf->rhf", out_grad, low[:, 2], preferred_element_type=jnp.float32
        )
        gate_grad = (hidden_grad * up_proj * slope_value).astype(jnp.bfloat16)
        up_grad = (hidden_grad * activated_hidden).astype(jnp.bfloat16)
        gradients = jnp.stack(
            [
                jnp.einsum("rhd,rhf->hdf", key_rows, gate_grad, preferred_element_type=jnp.float32),
                jnp.einsum("rhd,rhf->hdf", key_rows, up_grad, preferred_element_type=jnp.float32),
                jnp.einsum("rhd,rhf->hdf", out_grad, hidden, preferred_element_type=jnp.float32),
            ],
            axis=1,
        )
        total_grad = lax.psum(gradients, "seq")
        update = newton_schulz(total_grad, local_gram)
        weights = weights - LEARNING_STEP * update
        low = weights.astype(jnp.bfloat16)
        query_gate = jnp.einsum(
            "rhd,hdf->rhf", query_rows, low[:, 0], preferred_element_type=jnp.float32
        )
        query_up = jnp.einsum(
            "rhd,hdf->rhf", query_rows, low[:, 1], preferred_element_type=jnp.float32
        )
        query_act, unused_slope = silu_parts(query_gate)
        query_hidden = (query_act * query_up).astype(jnp.bfloat16)
        result = jnp.einsum(
            "rhf,hdf->rhd", query_hidden, low[:, 2], preferred_element_type=jnp.float32
        )
        results.append(result.astype(jnp.bfloat16).reshape(row_count, head_count * head_size))
    return jnp.stack(results)


def solution(mesh):
    return jax.shard_map(
        local,
        mesh=mesh,
        in_specs=(
            P(None, ("seq", "head"), None),
            P(None, ("seq", "head"), None),
            P(None, ("seq", "head"), None),
            P(None, ("seq", "head"), None),
            P("head", None, "seq", None),
        ),
        out_specs=P(None, "seq", "head"),
        check_vma=False,
    )
```

profile of v0, /device:TPU:0, one launch (start us, length us, event | category | flops | bytes accessed | tf_op | source)
XLA Modules:
  0.0 496.7 jit_solution(14485534307048518920)
XLA Ops:
  6.5 1.8 copy.62
  8.4 1.3 fusion.99
  9.7 4.3 all-to-all-start
  16.0 1.7 all-to-all-done
  17.7 3.5 all-to-all-start.2
  22.2 4.1 all-to-all-done.2
  26.4 3.4 all-to-all-start.1
  30.1 4.8 all-to-all-done.1
  35.5 38.2 %all-gather.2.cloned.1.call-done = f32[4,3,512,256]{3,2,0,1:T(8,128)} async-done(((f32[4,3,32,256]{3,2,0,1:T(8,128)}), f32[4,3,512,256]{3,2,0,1:T(8,128)}) %all-gather.2.cloned.1.call-update) | async-done | bytes 6291472 | tf_op jit(solution)/shard_map/all_gather | solution.py:41
  73.7 3.1 convert_element_type.105
  79.3 3.3 pad_maximum_fusion
  82.6 3.2 all-to-all-start.4
  87.8 1.6 all-to-all-done.4
  89.5 3.4 all-to-all-start.5
  93.0 5.1 %all-to-all-done.5 = bf16[32,2,2048]{2,0,1:T(8,128)(2,1)S(1)} async-done(((bf16[32,2,2048]{2,0,1:T(8,128)(2,1)}), bf16[32,2,2048]{2,0,1:T(8,128)(2,1)S(1)}, u32[]{:S(2)}, u32[]{:S(2)}) %all-to-all-start.5) | async-done | bytes 262176 | tf_op jit(solution)/shard_map/all_to_all | solution.py:49
  98.1 3.4 all-to-all-start.6
  102.2 4.5 all-to-all-done.6
  108.5 112.3 %all-reduce.3.cloned.1.call-done = f32[4,3,512,256]{2,3,0,1:T(8,128)} async-done(((f32[4,3,512,256]{2,3,0,1:T(8,128)}), f32[4,3,512,256]{2,3,0,1:T(8,128)}) %all-reduce.3.cloned.1.call-update) | async-done | bytes 6291472 | tf_op jit(solution)/shard_map/psum | solution.py:81
  220.8 19.0 %select_reduce_fusion.1 = (f32[4,3]{1,0:T(4,128)S(1)}, f32[4,3,256,256]{3,2,1,0:T(8,128)}) fusion(pred[256,256]{1,0:T(8,128)(4,1)S(1)} %iota_compare_fusion, f32[4,3,512,256]{2,3,0,1:T(8,128)} %all-reduce.3.cloned.1.call-done), kind=kOutput, calls=%fused_computation.31 | convolution fusion | flops 4833411072 | bytes 9502768 | tf_op jit(solution)/shard_map/hmrf,hmrg->hmfg/dot_general | solution.py:20
  239.9 6.4 %fusion.36 = f32[4,3,256,256]{3,2,1,0:T(8,128)S(1)} fusion(f32[4,3,256,256]{3,2,1,0:T(8,128)} %get-tuple-element.18, f32[4,3]{1,0:T(4,128)S(1)} %get-tuple-element.15), kind=kOutput, calls=%fused_computation.46 | convolution fusion | flops 2416705536 | bytes 6291504 | tf_op jit(solution)/shard_map/hmfg,hmgk->hmfk/dot_general | solution.py:32
  246.4 10.8 %fusion.2 = f32[4,3,512,256]{3,2,1,0:T(8,128)S(1)} fusion(f32[4,3,256,256]{3,2,1,0:T(8,128)S(1)} %fusion.36, f32[256,256]{1,0:T(8,128)S(1)} %broadcast_select_fusion, f32[4,3,256,256]{3,2,1,0:T(8,128)S(1)} %copy-done.1, f32[4,3]{1,0:T(4,128)S(1)} %get-tuple-element.15, f32[4,3,512,256]{2,3,0,1:T(8,128)S(1)} %bitcast.117, f32[4,3]{0,1:T(4,128)S(1)} %copy.76), kind=kOutput, calls=%fused_computation.4 | convolution fusion | flops 4837343232 | bytes 19136608 | tf_op jit(solution)/shard_map/hmrf,hmfg->hmrg/dot_general | solution.py:34
  257.2 10.6 %fusion.101 = f32[4,3,256,256]{3,2,1,0:T(8,128)S(1)} fusion(f32[4,3,512,256]{3,2,1,0:T(8,128)S(1)} %fusion.2), kind=kOutput, calls=%fused_computation.145 | convolution fusion | flops 4831838208 | bytes 9437184 | tf_op jit(solution)/shard_map/hmrf,hmrg->hmfg/dot_general | solution.py:20
  267.9 3.9 multiply_add_fusion.1
  271.8 8.1 %fusion.100 = (bf16[4,3,512,256]{3,2,0,1:T(8,128)(2,1)S(1)}, f32[4,3,512,256]{3,2,0,1:T(8,128)}) fusion(f32[4,3,512,256]{3,2,0,1:T(8,128)S(1)} %bitcast.115, f32[4,3,256,256]{3,2,1,0:T(8,128)S(1)} %multiply_add_fusion.1, f32[4,3,512,256]{3,2,1,0:T(8,128)S(1)} %fusion.2), kind=kOutput, calls=%fused_computation.144 | convolution fusion | flops 4836556800 | bytes 25165824 | tf_op jit(solution)/shard_map/hmrf,hmfg->hmrg/dot_general | solution.py:34
  282.6 3.3 pad_maximum_fusion.1
  286.0 1.9 fusion.96
  287.9 1.9 all_to_all.95
  289.7 1.7 copy.80
  291.5 4.1 all-to-all-start.3
  295.6 1.9 all_to_all.105
  297.4 1.7 copy.101
  299.1 1.7 all-to-all-done.3
  300.9 4.1 all-to-all-start.7
  305.0 1.9 reshape.93
  306.8 3.4 all-to-all-done.7
  310.2 1.8 reshape.95
  312.1 2.0 convolution_bitcast_fusion.12
  314.0 2.4 fusion.38
  316.4 1.2 copy.83
  318.4 107.0 %all-reduce.5.cloned.1.call-done = f32[4,3,512,256]{2,3,0,1:T(8,128)} async-done(((f32[4,3,512,256]{2,3,0,1:T(8,128)}), f32[4,3,512,256]{2,3,0,1:T(8,128)}) %all-reduce.5.cloned.1.call-update) | async-done | bytes 6291472 | tf_op jit(solution)/shard_map/psum | solution.py:81
  425.5 18.8 %select_reduce_fusion = (f32[4,3]{1,0:T(4,128)S(1)}, f32[4,3,256,256]{3,2,1,0:T(8,128)}) fusion(pred[256,256]{1,0:T(8,128)(4,1)S(1)} %iota_compare_fusion, f32[4,3,512,256]{2,3,0,1:T(8,128)} %all-reduce.5.cloned.1.call-done), kind=kOutput, calls=%fused_computation.24 | convolution fusion | flops 4833411072 | bytes 9502768 | tf_op jit(solution)/shard_map/hmrf,hmrg->hmfg/dot_general | solution.py:20
  444.4 6.7 %fusion.37 = f32[4,3,256,256]{3,2,1,0:T(8,128)S(1)} fusion(f32[4,3,256,256]{3,2,1,0:T(8,128)} %get-tuple-element.22, f32[4,3]{1,0:T(4,128)S(1)} %get-tuple-element.13), kind=kOutput, calls=%fused_computation.47 | convolution fusion | flops 2416705536 | bytes 6291504 | tf_op jit(solution)/shard_map/hmfg,hmgk->hmfk/dot_general | solution.py:32
  451.1 11.4 %fusion = f32[4,3,512,256]{3,2,1,0:T(8,128)S(1)} fusion(f32[4,3,256,256]{3,2,1,0:T(8,128)S(1)} %fusion.37, f32[256,256]{1,0:T(8,128)S(1)} %broadcast_select_fusion, f32[4,3,256,256]{3,2,1,0:T(8,128)S(1)} %copy-done, f32[4,3]{1,0:T(4,128)S(1)} %get-tuple-element.13, f32[4,3,512,256]{2,3,0,1:T(8,128)S(1)} %bitcast.119, f32[4,3]{0,1:T(4,128)S(1)} %copy.97), kind=kOutput, calls=%fused_computation.2 | convolution fusion | flops 4837343232 | bytes 19136608 | tf_op jit(solution)/shard_map/hmrf,hmfg->hmrg/dot_general | solution.py:34
  462.6 10.8 %fusion.102 = f32[4,3,256,256]{3,2,1,0:T(8,128)S(1)} fusion(f32[4,3,512,256]{3,2,1,0:T(8,128)S(1)} %fusion), kind=kOutput, calls=%fused_computation.146 | convolution fusion | flops 4831838208 | bytes 9437184 | tf_op jit(solution)/shard_map/hmrf,hmrg->hmfg/dot_general | solution.py:20
  473.4 4.1 multiply_add_fusion
  477.6 6.5 %subtract_convert_fusion = bf16[4,3,512,256]{3,2,0,1:T(8,128)(2,1)S(1)} fusion(f32[4,3,512,256]{3,2,0,1:T(8,128)S(1)} %bitcast.113, f32[4,3,256,256]{3,2,1,0:T(8,128)S(1)} %multiply_add_fusion, f32[4,3,512,256]{3,2,1,0:T(8,128)S(1)} %fusion), kind=kOutput, calls=%fused_computation.14 | convolution fusion | flops 4836556800 | bytes 18874368 | tf_op jit(solution)/shard_map/hmrf,hmfg->hmrg/dot_general | solution.py:34
  485.2 2.4 fusion.39
  487.5 1.2 copy.104
  (84 shorter events, 16.8 us)
Async XLA Ops:
  6.5 14.7 %copy-start.5 = (bf16[2,32,4096]{2,1,0:T(8,128)(2,1)S(1)}, bf16[2,32,4096]{2,1,0:T(8,128)(2,1)}, u32[]{:S(2)}) copy-start(bf16[2,32,4096]{2,1,0:T(8,128)(2,1)} %param.7) | copy-start | bytes 1572868
  6.5 67.2 %all-gather.2.cloned.1.call-start = ((), (), s32[]{:S(2)}) async-start(), calls=%async_computation.8 | async-start | bytes 6684672 | tf_op jit(solution)/shard_map/all_gather | solution.py:41
  9.7 8.0 %all-to-all-start = ((bf16[32,2,4]{0,2,1:T(4,128)(2,1)}), bf16[32,2,4]{0,2,1:T(4,128)(2,1)S(1)}, u32[]{:S(2)}, u32[]{:S(2)}) async-start(bf16[32,2,4]{0,2,1:T(4,128)(2,1)} %bitcast), calls=%async_computation | async-start | bytes 4096 | tf_op jit(solution)/shard_map/all_to_all | solution.py:50
  17.7 8.6 %all-to-all-start.2 = ((bf16[32,2,2048]{2,0,1:T(8,128)(2,1)}), bf16[32,2,2048]{2,0,1:T(8,128)(2,1)S(1)}, u32[]{:S(2)}, u32[]{:S(2)}) async-start(bf16[32,2,2048]{2,0,1:T(8,128)(2,1)} %copy.67), calls=%async_computation.2 | async-start | bytes 524288 | tf_op jit(solution)/shard_map/all_to_all | solution.py:48
  26.4 8.6 %all-to-all-start.1 = ((bf16[32,2,2048]{2,0,1:T(8,128)(2,1)}), bf16[32,2,2048]{2,0,1:T(8,128)(2,1)S(1)}, u32[]{:S(2)}, u32[]{:S(2)}) async-start(bf16[32,2,2048]{2,0,1:T(8,128)(2,1)} %copy.65), calls=%async_computation.1 | async-start | bytes 524288 | tf_op jit(solution)/shard_map/all_to_all | solution.py:49
  29.8 191.0 %all-reduce.3.cloned.1.call-start = ((), (), s32[]{:S(2)}) async-start(), calls=%async_computation.9 | async-start | bytes 12582912 | tf_op jit(solution)/shard_map/psum | solution.py:81
  82.6 6.8 %all-to-all-start.4 = ((bf16[32,2,4]{0,2,1:T(4,128)(2,1)}), bf16[32,2,4]{0,2,1:T(4,128)(2,1)S(1)}, u32[]{:S(2)}, u32[]{:S(2)}) async-start(bf16[32,2,4]{0,2,1:T(4,128)(2,1)} %bitcast.23), calls=%async_computation.4 | async-start | bytes 4096 | tf_op jit(solution)/shard_map/all_to_all | solution.py:50
  89.5 8.6 %all-to-all-start.5 = ((bf16[32,2,2048]{2,0,1:T(8,128)(2,1)}), bf16[32,2,2048]{2,0,1:T(8,128)(2,1)S(1)}, u32[]{:S(2)}, u32[]{:S(2)}) async-start(bf16[32,2,2048]{2,0,1:T(8,128)(2,1)} %copy.86), calls=%async_computation.5 | async-start | bytes 524288 | tf_op jit(solution)/shard_map/all_to_all | solution.py:49
  98.1 8.6 %all-to-all-start.6 = ((bf16[32,2,2048]{2,0,1:T(8,128)(2,1)}), bf16[32,2,2048]{2,0,1:T(8,128)(2,1)S(1)}, u32[]{:S(2)}, u32[]{:S(2)}) async-start(bf16[32,2,2048]{2,0,1:T(8,128)(2,1)} %copy.88), calls=%async_computation.6 | async-start | bytes 524288 | tf_op jit(solution)/shard_map/all_to_all | solution.py:48
  101.5 324.0 %all-reduce.5.cloned.1.call-start = ((), (), s32[]{:S(2)}) async-start(), calls=%async_computation.10 | async-start | bytes 12582912 | tf_op jit(solution)/shard_map/psum | solution.py:81
  220.8 25.5 %slice-start.4 = ((s8[6291456]{0:T(1024)(128)(4,1)}), s8[2097152]{0:T(1024)(128)(4,1)S(1)}, s32[]{:S(2)}) async-start(s8[6291456]{0:T(1024)(128)(4,1)} %bitcast.116), calls=%async_computation.15 | async-start | bytes 4194304
  239.9 6.4 %slice-start.5 = ((s8[6291456]{0:T(1024)(128)(4,1)}), s8[4194304]{0:T(1024)(128)(4,1)S(1)}, s32[]{:S(2)}) async-start(s8[6291456]{0:T(1024)(128)(4,1)} %bitcast.116), calls=%async_computation.16 | async-start | bytes 8388608
  239.9 6.4 %copy-start.1 = (f32[4,3,256,256]{3,2,1,0:T(8,128)S(1)}, f32[4,3,256,256]{3,2,1,0:T(8,128)}, u32[]{:S(2)}) copy-start(f32[4,3,256,256]{3,2,1,0:T(8,128)} %get-tuple-element.18) | copy-start | bytes 9437188
  239.9 31.8 %slice-start.2 = ((s8[6291456]{0:T(1024)(128)(4,1)}), s8[4194304]{0:T(1024)(128)(4,1)S(1)}, s32[]{:S(2)}) async-start(s8[6291456]{0:T(1024)(128)(4,1)} %bitcast.114), calls=%async_computation.13 | async-start | bytes 8388608
  246.4 25.4 %slice-start.3 = ((s8[6291456]{0:T(1024)(128)(4,1)}), s8[2097152]{0:T(1024)(128)(4,1)S(1)}, s32[]{:S(2)}) async-start(s8[6291456]{0:T(1024)(128)(4,1)} %bitcast.114), calls=%async_computation.14 | async-start | bytes 4194304
  271.8 8.1 %copy-start.2 = (bf16[64,4,512]{2,1,0:T(4,128)(2,1)S(1)}, bf16[64,4,512]{2,1,0:T(4,128)(2,1)}, u32[]{:S(2)}) copy-start(bf16[64,4,512]{2,1,0:T(4,128)(2,1)} %reshape.94) | copy-start | bytes 786436
  279.9 0.9 copy-start.4
  291.5 9.4 %all-to-all-start.3 = ((bf16[32,2,2048]{2,0,1:T(8,128)(2,1)}), bf16[32,2,2048]{2,0,1:T(8,128)(2,1)}, u32[]{:S(2)}, u32[]{:S(2)}) async-start(bf16[32,2,2048]{2,0,1:T(8,128)(2,1)} %copy.80), calls=%async_computation.3 | async-start | bytes 524288 | tf_op jit(solution)/shard_map/all_to_all | solution.py:47
  300.9 9.4 %all-to-all-start.7 = ((bf16[32,2,2048]{2,0,1:T(8,128)(2,1)}), bf16[32,2,2048]{2,0,1:T(8,128)(2,1)}, u32[]{:S(2)}, u32[]{:S(2)}) async-start(bf16[32,2,2048]{2,0,1:T(8,128)(2,1)} %copy.101), calls=%async_computation.7 | async-start | bytes 524288 | tf_op jit(solution)/shard_map/all_to_all | solution.py:47
  425.5 25.6 %slice-start.6 = ((s8[6291456]{0:T(1024)(128)(4,1)}), s8[2097152]{0:T(1024)(128)(4,1)S(1)}, s32[]{:S(2)}) async-start(s8[6291456]{0:T(1024)(128)(4,1)} %bitcast.118), calls=%async_computation.17 | async-start | bytes 4194304
  444.4 6.7 %slice-start.7 = ((s8[6291456]{0:T(1024)(128)(4,1)}), s8[4194304]{0:T(1024)(128)(4,1)S(1)}, s32[]{:S(2)}) async-start(s8[6291456]{0:T(1024)(128)(4,1)} %bitcast.118), calls=%async_computation.18 | async-start | bytes 8388608
  444.4 6.7 %copy-start = (f32[4,3,256,256]{3,2,1,0:T(8,128)S(1)}, f32[4,3,256,256]{3,2,1,0:T(8,128)}, u32[]{:S(2)}) copy-start(f32[4,3,256,256]{3,2,1,0:T(8,128)} %get-tuple-element.22) | copy-start | bytes 9437188
  444.4 33.2 %slice-start = ((s8[6291456]{0:T(1024)(128)(4,1)}), s8[4194304]{0:T(1024)(128)(4,1)S(1)}, s32[]{:S(2)}) async-start(s8[6291456]{0:T(1024)(128)(4,1)} %bitcast.112), calls=%async_computation.11 | async-start | bytes 8388608
  451.1 26.4 %slice-start.1 = ((s8[6291456]{0:T(1024)(128)(4,1)}), s8[2097152]{0:T(1024)(128)(4,1)S(1)}, s32[]{:S(2)}) async-start(s8[6291456]{0:T(1024)(128)(4,1)} %bitcast.112), calls=%async_computation.12 | async-start | bytes 4194304
  477.6 6.6 %copy-start.6 = (bf16[64,4,512]{2,1,0:T(4,128)(2,1)S(1)}, bf16[64,4,512]{2,1,0:T(4,128)(2,1)}, u32[]{:S(2)}) copy-start(bf16[64,4,512]{2,1,0:T(4,128)(2,1)} %reshape.95) | copy-start | bytes 786436
  484.1 4.7 copy-start.3
Sparse Core Ops, SparseCore 0:
  9.5 64.1 all-gather.1
  82.7 137.9 all-reduce.2
  286.1 139.3 all-reduce.4
where the time goes:
time: 502 us; the launch traced here: 497 us
  waiting for transfers between devices  285 us (57%)
  matrix products  130 us (26%)
  starting transfers between devices  29.8 us (6%)
  local copies, waits for them, and re-layouts  26.7 us (5%)
  between operations  14.1 us (3%)
  other arithmetic  11.8 us (2%)
    psum x2, waiting for transfers between devices, local(): total_grad = lax.psum(gradients, 'seq')  219 us
    dot_general x4, matrix products, local_gram(): jnp.einsum('hmrf,hmrg->hmfg', weight_matrices, weight_matrices, precision...  59.2 us
    all_gather x1, waiting for transfers between devices, local(): weights = lax.all_gather(fast_init, 'seq', axis=2, tiled=True)  38.2 us
    dot_general x4, matrix products, newton_schulz(): jnp.einsum('hmrf,hmfg->hmrg', current_weights, polynomial_update, precisi...  36.9 us
    dot_general x4, matrix products, newton_schulz(): jnp.einsum('hmfg,hmgk->hmfk', gram_matrix, gram_matrix, precision=FULL_PR...  21.1 us
  transfers between devices with their start and end apart: 11, of which 11 were waited for; matrix products, arithmetic and copies ran while one was open for 5% of the time, Pallas kernels for 0%

commit v1 on v0

--- a/solution.py
+++ b/solution.py
@@ -38,7 +38,21 @@
 
 
 def local(queries, keys, values, rates, fast_init):
-    weights = lax.all_gather(fast_init, "seq", axis=2, tiled=True)
+    ways, here, hop = (lax.axis_size("seq"), lax.axis_index("seq"), fast_init.shape[2])
+    dims = [n * ways if d == 2 else n for d, n in enumerate(fast_init.shape)]
+    full = lax.dynamic_update_slice_in_dim(
+        jnp.zeros(dims, fast_init.dtype), fast_init, here * hop, axis=2
+    )
+    going_up = going_down = fast_init
+    for far in range(1, ways // 2 + 1):
+        going_up = lax.ppermute(going_up, "seq", [(d, (d + 1) % ways) for d in range(ways)])
+        full = lax.dynamic_update_slice_in_dim(full, going_up, (here - far) % ways * hop, axis=2)
+        if 2 * far < ways:
+            going_down = lax.ppermute(going_down, "seq", [(d, (d - 1) % ways) for d in range(ways)])
+            full = lax.dynamic_update_slice_in_dim(
+                full, going_down, (here + far) % ways * hop, axis=2
+            )
+    weights = full
     head_count = weights.shape[0]
     head_size = weights.shape[2]
     results = []

time: 502 us -> 537 us (1.070)
  starting transfers between devices: 29.8 us -> 64 us
  waiting for transfers between devices: 285 us -> 264 us
  local copies, waits for them, and re-layouts: 26.7 us -> 44.1 us
    all_gather x1 -> x0, waiting for transfers between devices: 38.2 us -> none  [local(): weights = lax.all_gather(fast_init, 'seq', axis=2, tiled=True)]
    ppermute x0 -> x15, starting transfers between devices: none -> 35.3 us  [the longest x7 29.2 us: local(): lax.ppermute(going_down, 'seq', [(d, (d - 1) % ways) for d in range(ways)])]
    ppermute x0 -> x15, waiting for transfers between devices: none -> 18.6 us  [the longest x8 16.8 us: local(): lax.ppermute(going_up, 'seq', [(d, (d + 1) % ways) for d in range(ways)])]
    dynamic_update_slice x0 -> x15, local copies, waits for them, and re-layouts: none -> 16.8 us  [the longest x7 8.5 us: local(): lax.dynamic_update_slice_in_dim(full, going_down, (here + far) % ways * h...]
  transfers between devices with their start and end apart: 11 -> 25, of which waited for: 11 -> 14; matrix products, arithmetic and copies ran while one was open for 5% -> 7% of each run, Pallas kernels for 0% -> 0%
where the time goes in v1:
time: 537 us; the launch traced here: 530 us
  waiting for transfers between devices  264 us (49%)
  matrix products  132 us (25%)
  starting transfers between devices  64 us (12%)
  local copies, waits for them, and re-layouts  44.1 us (8%)
  between operations  14.6 us (3%)
  other arithmetic  11.9 us (2%)
    psum x2, waiting for transfers between devices, local(): total_grad = lax.psum(gradients, 'seq')  224 us
    dot_general x4, matrix products, local_gram(): jnp.einsum('hmrf,hmrg->hmfg', weight_matrices, weight_matrices, precision...  59.2 us
    dot_general x4, matrix products, newton_schulz(): jnp.einsum('hmrf,hmfg->hmrg', current_weights, polynomial_update, precisi...  38.8 us
    ppermute x7, starting transfers between devices, local(): lax.ppermute(going_down, 'seq', [(d, (d - 1) % ways) for d in range(ways)])  29.2 us
    dot_general x4, matrix products, newton_schulz(): jnp.einsum('hmfg,hmgk->hmfk', gram_matrix, gram_matrix, precision=FULL_PR...  21.1 us
    ppermute x8, waiting for transfers between devices, local(): lax.ppermute(going_up, 'seq', [(d, (d + 1) % ways) for d in range(ways)])  16.8 us
  transfers between devices with their start and end apart: 25, of which 14 were waited for; matrix products, arithmetic and copies ran while one was open for 7% of the time, Pallas kernels for 0%

profile of v1, /device:TPU:0, one launch (start us, length us, event | category | flops | bytes accessed | tf_op | source)
XLA Modules:
  0.0 530.0 jit_solution(6141894584587948797)
XLA Ops:
  6.5 3.2 broadcast_in_dim.26
  11.2 4.9 collective-permute-start.1
  16.6 3.3 all-to-all-start
  22.6 3.4 collective-permute-start.3
  26.1 5.5 %collective-permute-done.2 = f32[4,3,32,256]{3,2,0,1:T(8,128)S(1)} collective-permute-done((f32[4,3,32,256]{3,2,0,1:T(8,128)S(1)}, f32[4,3,32,256]{3,2,0,1:T(8,128)S(1)}, u32[]{:S(2)}, u32[]{:S(2)}) %collective-permute-start.2) | collective-permute-done | bytes 393248 | tf_op jit(solution)/shard_map/ppermute | solution.py:48
  31.6 2.0 collective-permute-start.4
  33.6 2.6 collective-permute-start.5
  38.4 3.4 all-to-all-start.1
  42.0 2.5 collective-permute-start.6
  44.4 4.3 collective-permute-start.7
  48.8 3.4 all-to-all-start.2
  52.7 4.7 all-to-all-done.2
  58.6 5.1 collective-permute-start.9
  64.5 3.9 collective-permute-done.8
  72.8 4.5 collective-permute-start.11
  83.4 4.4 collective-permute-start.13
  93.9 5.2 collective-permute-done.14
  99.9 3.1 convert_element_type.98
  105.5 3.4 pad_maximum_fusion
  108.9 3.2 all-to-all-start.4
  115.9 3.5 all-to-all-start.5
  119.5 5.1 all-to-all-done.5
  124.5 3.4 all-to-all-start.6
  128.7 4.5 all-to-all-done.6
  134.9 117.1 %all-reduce.3.cloned.1.call-done = f32[4,3,512,256]{2,3,0,1:T(8,128)} async-done(((f32[4,3,512,256]{2,3,0,1:T(8,128)}), f32[4,3,512,256]{2,3,0,1:T(8,128)}) %all-reduce.3.cloned.1.call-update) | async-done | bytes 6291472 | tf_op jit(solution)/shard_map/psum | solution.py:95
  252.0 19.0 %select_reduce_fusion.1 = (f32[4,3]{1,0:T(4,128)S(1)}, f32[4,3,256,256]{3,2,1,0:T(8,128)}) fusion(pred[256,256]{1,0:T(8,128)(4,1)S(1)} %iota_compare_fusion, f32[4,3,512,256]{2,3,0,1:T(8,128)} %all-reduce.3.cloned.1.call-done), kind=kOutput, calls=%fused_computation.31 | convolution fusion | flops 4833411072 | bytes 9502768 | tf_op jit(solution)/shard_map/hmrf,hmrg->hmfg/dot_general | solution.py:20
  271.1 6.4 %fusion.36 = f32[4,3,256,256]{3,2,1,0:T(8,128)S(1)} fusion(f32[4,3,256,256]{3,2,1,0:T(8,128)} %get-tuple-element.20, f32[4,3]{1,0:T(4,128)S(1)} %get-tuple-element.17), kind=kOutput, calls=%fused_computation.46 | convolution fusion | flops 2416705536 | bytes 6291504 | tf_op jit(solution)/shard_map/hmfg,hmgk->hmfk/dot_general | solution.py:32
  277.6 10.8 %fusion.2 = f32[4,3,512,256]{3,2,1,0:T(8,128)S(1)} fusion(f32[4,3,256,256]{3,2,1,0:T(8,128)S(1)} %fusion.36, f32[256,256]{1,0:T(8,128)S(1)} %broadcast_select_fusion, f32[4,3,256,256]{3,2,1,0:T(8,128)S(1)} %copy-done.1, f32[4,3]{1,0:T(4,128)S(1)} %get-tuple-element.17, f32[4,3,512,256]{2,3,0,1:T(8,128)S(1)} %bitcast.115, f32[4,3]{0,1:T(4,128)S(1)} %copy.82), kind=kOutput, calls=%fused_computation.4 | convolution fusion | flops 4837343232 | bytes 19136608 | tf_op jit(solution)/shard_map/hmrf,hmfg->hmrg/dot_general | solution.py:34
  288.4 10.6 %fusion.102 = f32[4,3,256,256]{3,2,1,0:T(8,128)S(1)} fusion(f32[4,3,512,256]{3,2,1,0:T(8,128)S(1)} %fusion.2), kind=kOutput, calls=%fused_computation.162 | convolution fusion | flops 4831838208 | bytes 9437184 | tf_op jit(solution)/shard_map/hmrf,hmrg->hmfg/dot_general | solution.py:20
  299.0 3.9 multiply_add_fusion.1
  302.9 10.0 %fusion.101 = (bf16[4,3,512,256]{3,2,0,1:T(8,128)(2,1)S(1)}, f32[4,3,512,256]{3,2,0,1:T(8,128)}) fusion(f32[4,3,512,256]{3,2,0,1:T(8,128)} %constant_dynamic-update-slice_fusion, f32[4,3,256,256]{3,2,1,0:T(8,128)S(1)} %multiply_add_fusion.1, f32[4,3,512,256]{3,2,1,0:T(8,128)S(1)} %fusion.2), kind=kOutput, calls=%fused_computation.161 | convolution fusion | flops 4836556800 | bytes 25165824 | tf_op jit(solution)/shard_map/hmrf,hmfg->hmrg/dot_general | solution.py:34
  315.7 3.3 pad_maximum_fusion.1
  319.1 1.9 fusion.96
  320.9 1.9 all_to_all.95
  324.5 4.1 all-to-all-start.3
  328.6 1.9 all_to_all.105
  333.9 4.1 all-to-all-start.7
  339.9 3.4 all-to-all-done.7
  345.1 2.0 convolution_bitcast_fusion.12
  347.1 2.4 fusion.38
  351.5 107.0 %all-reduce.5.cloned.1.call-done = f32[4,3,512,256]{2,3,0,1:T(8,128)} async-done(((f32[4,3,512,256]{2,3,0,1:T(8,128)}), f32[4,3,512,256]{2,3,0,1:T(8,128)}) %all-reduce.5.cloned.1.call-update) | async-done | bytes 6291472 | tf_op jit(solution)/shard_map/psum | solution.py:95
  458.6 18.7 %select_reduce_fusion = (f32[4,3]{1,0:T(4,128)S(1)}, f32[4,3,256,256]{3,2,1,0:T(8,128)}) fusion(pred[256,256]{1,0:T(8,128)(4,1)S(1)} %iota_compare_fusion, f32[4,3,512,256]{2,3,0,1:T(8,128)} %all-reduce.5.cloned.1.call-done), kind=kOutput, calls=%fused_computation.24 | convolution fusion | flops 4833411072 | bytes 9502768 | tf_op jit(solution)/shard_map/hmrf,hmrg->hmfg/dot_general | solution.py:20
  477.4 6.7 %fusion.37 = f32[4,3,256,256]{3,2,1,0:T(8,128)S(1)} fusion(f32[4,3,256,256]{3,2,1,0:T(8,128)} %get-tuple-element.24, f32[4,3]{1,0:T(4,128)S(1)} %get-tuple-element.15), kind=kOutput, calls=%fused_computation.47 | convolution fusion | flops 2416705536 | bytes 6291504 | tf_op jit(solution)/shard_map/hmfg,hmgk->hmfk/dot_general | solution.py:32
  484.2 11.4 %fusion = f32[4,3,512,256]{3,2,1,0:T(8,128)S(1)} fusion(f32[4,3,256,256]{3,2,1,0:T(8,128)S(1)} %fusion.37, f32[256,256]{1,0:T(8,128)S(1)} %broadcast_select_fusion, f32[4,3,256,256]{3,2,1,0:T(8,128)S(1)} %copy-done, f32[4,3]{1,0:T(4,128)S(1)} %get-tuple-element.15, f32[4,3,512,256]{2,3,0,1:T(8,128)S(1)} %bitcast.117, f32[4,3]{0,1:T(4,128)S(1)} %copy.103), kind=kOutput, calls=%fused_computation.2 | convolution fusion | flops 4837343232 | bytes 19136608 | tf_op jit(solution)/shard_map/hmrf,hmfg->hmrg/dot_general | solution.py:34
  495.6 10.8 %fusion.103 = f32[4,3,256,256]{3,2,1,0:T(8,128)S(1)} fusion(f32[4,3,512,256]{3,2,1,0:T(8,128)S(1)} %fusion), kind=kOutput, calls=%fused_computation.163 | convolution fusion | flops 4831838208 | bytes 9437184 | tf_op jit(solution)/shard_map/hmrf,hmrg->hmfg/dot_general | solution.py:20
  506.5 4.1 multiply_add_fusion
  510.6 6.5 %subtract_convert_fusion = bf16[4,3,512,256]{3,2,0,1:T(8,128)(2,1)S(1)} fusion(f32[4,3,512,256]{3,2,0,1:T(8,128)S(1)} %bitcast.113, f32[4,3,256,256]{3,2,1,0:T(8,128)S(1)} %multiply_add_fusion, f32[4,3,512,256]{3,2,1,0:T(8,128)S(1)} %fusion), kind=kOutput, calls=%fused_computation.14 | convolution fusion | flops 4836556800 | bytes 18874368 | tf_op jit(solution)/shard_map/hmrf,hmfg->hmrg/dot_general | solution.py:34
  518.2 2.4 fusion.39
  (128 shorter events, 52.5 us)
Async XLA Ops:
  6.5 3.2 copy-start.7
  6.5 9.5 %copy-start.9 = (bf16[2,32,8]{1,2,0:T(8,128)(2,1)S(1)}, bf16[2,32,8]{1,2,0:T(8,128)(2,1)}, u32[]{:S(2)}) copy-start(bf16[2,32,8]{1,2,0:T(8,128)(2,1)} %param.8) | copy-start | bytes 3076
  6.5 19.5 %copy-start.5 = (bf16[2,32,4096]{2,1,0:T(8,128)(2,1)S(1)}, bf16[2,32,4096]{2,1,0:T(8,128)(2,1)}, u32[]{:S(2)}) copy-start(bf16[2,32,4096]{2,1,0:T(8,128)(2,1)} %param.7) | copy-start | bytes 1572868
  6.5 29.6 %copy-start.6 = (bf16[2,32,4096]{2,1,0:T(8,128)(2,1)S(1)}, bf16[2,32,4096]{2,1,0:T(8,128)(2,1)}, u32[]{:S(2)}) copy-start(bf16[2,32,4096]{2,1,0:T(8,128)(2,1)} %param.6) | copy-start | bytes 1572868
  10.6 11.0 %collective-permute-start = (f32[4,3,32,256]{3,2,0,1:T(8,128)S(1)}, f32[4,3,32,256]{3,2,0,1:T(8,128)S(1)}, u32[]{:S(2)}, u32[]{:S(2)}) collective-permute-start(f32[4,3,32,256]{3,2,0,1:T(8,128)S(1)} %get-tuple-element.11), channel_id=1, source_target_pairs={{0,2},{2,4},{4,6},{6,8},{8,10},{10,12},{12,14},{14,16},{16,18},{18... | collective-permute-start | bytes 1179656 | tf_op jit(solution)/shard_map/ppermute | solution.py:48
  11.2 11.5 %collective-permute-start.1 = (f32[4,3,32,256]{3,2,0,1:T(8,128)S(1)}, f32[4,3,32,256]{3,2,0,1:T(8,128)S(1)}, u32[]{:S(2)}, u32[]{:S(2)}) collective-permute-start(f32[4,3,32,256]{3,2,0,1:T(8,128)S(1)} %get-tuple-element.11), channel_id=1, source_target_pairs={{0,30},{2,0},{4,2},{6,4},{8,6},{10,8},{12,10},{14,12},{16,14},{18,... | collective-permute-start | bytes 1179656 | tf_op jit(solution)/shard_map/ppermute | solution.py:51
  16.6 21.8 %all-to-all-start = ((bf16[32,2,4]{0,2,1:T(4,128)(2,1)}), bf16[32,2,4]{0,2,1:T(4,128)(2,1)S(1)}, u32[]{:S(2)}, u32[]{:S(2)}) async-start(bf16[32,2,4]{0,2,1:T(4,128)(2,1)} %bitcast.1), calls=%async_computation | async-start | bytes 4096 | tf_op jit(solution)/shard_map/all_to_all | solution.py:64
  21.6 10.0 %collective-permute-start.2 = (f32[4,3,32,256]{3,2,0,1:T(8,128)S(1)}, f32[4,3,32,256]{3,2,0,1:T(8,128)S(1)}, u32[]{:S(2)}, u32[]{:S(2)}) collective-permute-start(f32[4,3,32,256]{3,2,0,1:T(8,128)S(1)} %collective-permute-done), channel_id=1, source_target_pairs={{0,2},{2,4},{4,6},{6,8},{8,10},{10,12},{12,14},{14,16},{16,18},{18... | collective-permute-start | bytes 1179656 | tf_op jit(solution)/shard_map/ppermute | solution.py:48
  22.6 10.9 %collective-permute-start.3 = (f32[4,3,32,256]{3,2,0,1:T(8,128)S(1)}, f32[4,3,32,256]{3,2,0,1:T(8,128)}, u32[]{:S(2)}, u32[]{:S(2)}) collective-permute-start(f32[4,3,32,256]{3,2,0,1:T(8,128)S(1)} %collective-permute-done.1), channel_id=1, source_target_pairs={{0,30},{2,0},{4,2},{6,4},{8,6},{10,8},{12,10},{14,12},{16,14},{18,... | collective-permute-start | bytes 1179656 | tf_op jit(solution)/shard_map/ppermute | solution.py:51
  31.6 10.4 %collective-permute-start.4 = (f32[4,3,32,256]{3,2,0,1:T(8,128)S(1)}, f32[4,3,32,256]{3,2,0,1:T(8,128)}, u32[]{:S(2)}, u32[]{:S(2)}) collective-permute-start(f32[4,3,32,256]{3,2,0,1:T(8,128)S(1)} %collective-permute-done.2), channel_id=1, source_target_pairs={{0,2},{2,4},{4,6},{6,8},{8,10},{10,12},{12,14},{14,16},{16,18},{18... | collective-permute-start | bytes 1179656 | tf_op jit(solution)/shard_map/ppermute | solution.py:48
  33.6 10.8 %collective-permute-start.5 = (f32[4,3,32,256]{3,2,0,1:T(8,128)}, f32[4,3,32,256]{3,2,0,1:T(8,128)}, u32[]{:S(2)}, u32[]{:S(2)}) collective-permute-start(f32[4,3,32,256]{3,2,0,1:T(8,128)} %collective-permute-done.3), channel_id=1, source_target_pairs={{0,30},{2,0},{4,2},{6,4},{8,6},{10,8},{12,10},{14,12},{16,14},{18,... | collective-permute-start | bytes 1179656 | tf_op jit(solution)/shard_map/ppermute | solution.py:51
  38.4 10.4 %all-to-all-start.1 = ((bf16[32,2,2048]{2,0,1:T(8,128)(2,1)}), bf16[32,2,2048]{2,0,1:T(8,128)(2,1)S(1)}, u32[]{:S(2)}, u32[]{:S(2)}) async-start(bf16[32,2,2048]{2,0,1:T(8,128)(2,1)} %copy.71), calls=%async_computation.1 | async-start | bytes 524288 | tf_op jit(solution)/shard_map/all_to_all | solution.py:63
  42.0 15.6 %collective-permute-start.6 = (f32[4,3,32,256]{3,2,0,1:T(8,128)}, f32[4,3,32,256]{3,2,0,1:T(8,128)}, u32[]{:S(2)}, u32[]{:S(2)}) collective-permute-start(f32[4,3,32,256]{3,2,0,1:T(8,128)} %collective-permute-done.4), channel_id=1, source_target_pairs={{0,2},{2,4},{4,6},{6,8},{8,10},{10,12},{12,14},{14,16},{16,18},{18... | collective-permute-start | bytes 1179656 | tf_op jit(solution)/shard_map/ppermute | solution.py:48
  44.4 14.2 %collective-permute-start.7 = (f32[4,3,32,256]{3,2,0,1:T(8,128)}, f32[4,3,32,256]{3,2,0,1:T(8,128)}, u32[]{:S(2)}, u32[]{:S(2)}) collective-permute-start(f32[4,3,32,256]{3,2,0,1:T(8,128)} %collective-permute-done.5), channel_id=1, source_target_pairs={{0,30},{2,0},{4,2},{6,4},{8,6},{10,8},{12,10},{14,12},{16,14},{18,... | collective-permute-start | bytes 1179656 | tf_op jit(solution)/shard_map/ppermute | solution.py:51
  48.8 8.6 %all-to-all-start.2 = ((bf16[32,2,2048]{2,0,1:T(8,128)(2,1)}), bf16[32,2,2048]{2,0,1:T(8,128)(2,1)S(1)}, u32[]{:S(2)}, u32[]{:S(2)}) async-start(bf16[32,2,2048]{2,0,1:T(8,128)(2,1)} %copy.73), calls=%async_computation.2 | async-start | bytes 524288 | tf_op jit(solution)/shard_map/all_to_all | solution.py:62
  52.2 199.8 %all-reduce.3.cloned.1.call-start = ((), (), s32[]{:S(2)}) async-start(), calls=%async_computation.8 | async-start | bytes 12582912 | tf_op jit(solution)/shard_map/psum | solution.py:95
  57.6 10.9 %collective-permute-start.8 = (f32[4,3,32,256]{3,2,0,1:T(8,128)}, f32[4,3,32,256]{3,2,0,1:T(8,128)S(1)}, u32[]{:S(2)}, u32[]{:S(2)}) collective-permute-start(f32[4,3,32,256]{3,2,0,1:T(8,128)} %collective-permute-done.6), channel_id=1, source_target_pairs={{0,2},{2,4},{4,6},{6,8},{8,10},{10,12},{12,14},{14,16},{16,18},{18... | collective-permute-start | bytes 1179656 | tf_op jit(solution)/shard_map/ppermute | solution.py:48
  58.6 14.2 %collective-permute-start.9 = (f32[4,3,32,256]{3,2,0,1:T(8,128)}, f32[4,3,32,256]{3,2,0,1:T(8,128)S(1)}, u32[]{:S(2)}, u32[]{:S(2)}) collective-permute-start(f32[4,3,32,256]{3,2,0,1:T(8,128)} %collective-permute-done.7), channel_id=1, source_target_pairs={{0,30},{2,0},{4,2},{6,4},{8,6},{10,8},{12,10},{14,12},{16,14},{18,... | collective-permute-start | bytes 1179656 | tf_op jit(solution)/shard_map/ppermute | solution.py:51
  68.4 10.6 %collective-permute-start.10 = (f32[4,3,32,256]{3,2,0,1:T(8,128)S(1)}, f32[4,3,32,256]{3,2,0,1:T(8,128)S(1)}, u32[]{:S(2)}, u32[]{:S(2)}) collective-permute-start(f32[4,3,32,256]{3,2,0,1:T(8,128)S(1)} %collective-permute-done.8), channel_id=1, source_target_pairs={{0,2},{2,4},{4,6},{6,8},{8,10},{10,12},{12,14},{14,16},{16,18},{18... | collective-permute-start | bytes 1179656 | tf_op jit(solution)/shard_map/ppermute | solution.py:48
  72.8 10.6 %collective-permute-start.11 = (f32[4,3,32,256]{3,2,0,1:T(8,128)S(1)}, f32[4,3,32,256]{3,2,0,1:T(8,128)S(1)}, u32[]{:S(2)}, u32[]{:S(2)}) collective-permute-start(f32[4,3,32,256]{3,2,0,1:T(8,128)S(1)} %collective-permute-done.9), channel_id=1, source_target_pairs={{0,30},{2,0},{4,2},{6,4},{8,6},{10,8},{12,10},{14,12},{16,14},{18,... | collective-permute-start | bytes 1179656 | tf_op jit(solution)/shard_map/ppermute | solution.py:51
  79.0 10.0 %collective-permute-start.12 = (f32[4,3,32,256]{3,2,0,1:T(8,128)S(1)}, f32[4,3,32,256]{3,2,0,1:T(8,128)S(1)}, u32[]{:S(2)}, u32[]{:S(2)}) collective-permute-start(f32[4,3,32,256]{3,2,0,1:T(8,128)S(1)} %collective-permute-done.10), channel_id=1, source_target_pairs={{0,2},{2,4},{4,6},{6,8},{8,10},{10,12},{12,14},{14,16},{16,18},{18... | collective-permute-start | bytes 1179656 | tf_op jit(solution)/shard_map/ppermute | solution.py:48
  83.4 9.7 %collective-permute-start.13 = (f32[4,3,32,256]{3,2,0,1:T(8,128)S(1)}, f32[4,3,32,256]{3,2,0,1:T(8,128)S(1)}, u32[]{:S(2)}, u32[]{:S(2)}) collective-permute-start(f32[4,3,32,256]{3,2,0,1:T(8,128)S(1)} %collective-permute-done.11), channel_id=1, source_target_pairs={{0,30},{2,0},{4,2},{6,4},{8,6},{10,8},{12,10},{14,12},{16,14},{18,... | collective-permute-start | bytes 1179656 | tf_op jit(solution)/shard_map/ppermute | solution.py:51
  89.0 10.1 %collective-permute-start.14 = (f32[4,3,32,256]{3,2,0,1:T(8,128)S(1)}, f32[4,3,32,256]{3,2,0,1:T(8,128)S(1)}, u32[]{:S(2)}, u32[]{:S(2)}) collective-permute-start(f32[4,3,32,256]{3,2,0,1:T(8,128)S(1)} %collective-permute-done.12), channel_id=1, source_target_pairs={{0,2},{2,4},{4,6},{6,8},{8,10},{10,12},{12,14},{14,16},{16,18},{18... | collective-permute-start | bytes 1179656 | tf_op jit(solution)/shard_map/ppermute | solution.py:48
  108.9 6.9 %all-to-all-start.4 = ((bf16[32,2,4]{0,2,1:T(4,128)(2,1)}), bf16[32,2,4]{0,2,1:T(4,128)(2,1)S(1)}, u32[]{:S(2)}, u32[]{:S(2)}) async-start(bf16[32,2,4]{0,2,1:T(4,128)(2,1)} %bitcast.23), calls=%async_computation.4 | async-start | bytes 4096 | tf_op jit(solution)/shard_map/all_to_all | solution.py:64
  115.9 8.7 %all-to-all-start.5 = ((bf16[32,2,2048]{2,0,1:T(8,128)(2,1)}), bf16[32,2,2048]{2,0,1:T(8,128)(2,1)S(1)}, u32[]{:S(2)}, u32[]{:S(2)}) async-start(bf16[32,2,2048]{2,0,1:T(8,128)(2,1)} %copy.92), calls=%async_computation.5 | async-start | bytes 524288 | tf_op jit(solution)/shard_map/all_to_all | solution.py:63
  124.5 8.6 %all-to-all-start.6 = ((bf16[32,2,2048]{2,0,1:T(8,128)(2,1)}), bf16[32,2,2048]{2,0,1:T(8,128)(2,1)S(1)}, u32[]{:S(2)}, u32[]{:S(2)}) async-start(bf16[32,2,2048]{2,0,1:T(8,128)(2,1)} %copy.94), calls=%async_computation.6 | async-start | bytes 524288 | tf_op jit(solution)/shard_map/all_to_all | solution.py:62
  128.0 330.6 %all-reduce.5.cloned.1.call-start = ((), (), s32[]{:S(2)}) async-start(), calls=%async_computation.9 | async-start | bytes 12582912 | tf_op jit(solution)/shard_map/psum | solution.py:95
  252.0 25.5 %slice-start.2 = ((s8[6291456]{0:T(1024)(128)(4,1)}), s8[2097152]{0:T(1024)(128)(4,1)S(1)}, s32[]{:S(2)}) async-start(s8[6291456]{0:T(1024)(128)(4,1)} %bitcast.114), calls=%async_computation.12 | async-start | bytes 4194304
  271.1 6.4 %slice-start.3 = ((s8[6291456]{0:T(1024)(128)(4,1)}), s8[4194304]{0:T(1024)(128)(4,1)S(1)}, s32[]{:S(2)}) async-start(s8[6291456]{0:T(1024)(128)(4,1)} %bitcast.114), calls=%async_computation.13 | async-start | bytes 8388608
  271.1 6.4 %copy-start.1 = (f32[4,3,256,256]{3,2,1,0:T(8,128)S(1)}, f32[4,3,256,256]{3,2,1,0:T(8,128)}, u32[]{:S(2)}) copy-start(f32[4,3,256,256]{3,2,1,0:T(8,128)} %get-tuple-element.20) | copy-start | bytes 9437188
  302.9 10.1 %copy-start.2 = (bf16[64,4,512]{2,1,0:T(4,128)(2,1)S(1)}, bf16[64,4,512]{2,1,0:T(4,128)(2,1)}, u32[]{:S(2)}) copy-start(bf16[64,4,512]{2,1,0:T(4,128)(2,1)} %reshape.94) | copy-start | bytes 786436
  313.0 0.9 copy-start.4
  324.5 9.4 %all-to-all-start.3 = ((bf16[32,2,2048]{2,0,1:T(8,128)(2,1)}), bf16[32,2,2048]{2,0,1:T(8,128)(2,1)}, u32[]{:S(2)}, u32[]{:S(2)}) async-start(bf16[32,2,2048]{2,0,1:T(8,128)(2,1)} %copy.86), calls=%async_computation.3 | async-start | bytes 524288 | tf_op jit(solution)/shard_map/all_to_all | solution.py:61
  333.9 9.4 %all-to-all-start.7 = ((bf16[32,2,2048]{2,0,1:T(8,128)(2,1)}), bf16[32,2,2048]{2,0,1:T(8,128)(2,1)}, u32[]{:S(2)}, u32[]{:S(2)}) async-start(bf16[32,2,2048]{2,0,1:T(8,128)(2,1)} %copy.107), calls=%async_computation.7 | async-start | bytes 524288 | tf_op jit(solution)/shard_map/all_to_all | solution.py:61
  458.6 25.6 %slice-start.4 = ((s8[6291456]{0:T(1024)(128)(4,1)}), s8[2097152]{0:T(1024)(128)(4,1)S(1)}, s32[]{:S(2)}) async-start(s8[6291456]{0:T(1024)(128)(4,1)} %bitcast.116), calls=%async_computation.14 | async-start | bytes 4194304
  477.4 6.7 %slice-start.5 = ((s8[6291456]{0:T(1024)(128)(4,1)}), s8[4194304]{0:T(1024)(128)(4,1)S(1)}, s32[]{:S(2)}) async-start(s8[6291456]{0:T(1024)(128)(4,1)} %bitcast.116), calls=%async_computation.15 | async-start | bytes 8388608
  477.4 6.7 %copy-start = (f32[4,3,256,256]{3,2,1,0:T(8,128)S(1)}, f32[4,3,256,256]{3,2,1,0:T(8,128)}, u32[]{:S(2)}) copy-start(f32[4,3,256,256]{3,2,1,0:T(8,128)} %get-tuple-element.24) | copy-start | bytes 9437188
  477.4 33.2 %slice-start = ((s8[6291456]{0:T(1024)(128)(4,1)}), s8[4194304]{0:T(1024)(128)(4,1)S(1)}, s32[]{:S(2)}) async-start(s8[6291456]{0:T(1024)(128)(4,1)} %bitcast.112), calls=%async_computation.10 | async-start | bytes 8388608
  484.2 26.4 %slice-start.1 = ((s8[6291456]{0:T(1024)(128)(4,1)}), s8[2097152]{0:T(1024)(128)(4,1)S(1)}, s32[]{:S(2)}) async-start(s8[6291456]{0:T(1024)(128)(4,1)} %bitcast.112), calls=%async_computation.11 | async-start | bytes 4194304
  510.6 6.6 %copy-start.8 = (bf16[64,4,512]{2,1,0:T(4,128)(2,1)S(1)}, bf16[64,4,512]{2,1,0:T(4,128)(2,1)}, u32[]{:S(2)}) copy-start(bf16[64,4,512]{2,1,0:T(4,128)(2,1)} %reshape.95) | copy-start | bytes 786436
  517.2 4.7 copy-start.3
Sparse Core Ops, SparseCore 0:
  109.1 142.8 all-reduce.2
  319.2 139.3 all-reduce.4
